TPU v7x, 512 devices: a whole 4x4x16 slice. The times are simulated.
512 devices in a mesh: dp: 16 (over z), fsdp: 32 (over x, y, core).
Axes of the slice: x: 4, y: 4, z: 16, core: 2. Of those that a mesh axis runs over, the one named last changes fastest.
Arguments:
- txt_tokens: bfloat16 [512, 8, 3072], P(('dp', 'fsdp')), may hold values from -6 to 6
- concept_table: bfloat16 [4096, 3072], P('dp'), may hold values from -6 to 6
- concept_ids: int32 [512], P(('dp', 'fsdp')), may hold values from 0 to 4095
- positions: int32 [512], P(('dp', 'fsdp')), may hold values from 0 to 7
- timesteps: int32 [512], P(('dp', 'fsdp')), may hold values from 0 to 63
- counts: int32 [4096], P('dp'), may hold values from 1 to 16
- mod_table: bfloat16 [64, 2, 3072], P(None, None, 'fsdp'), may hold values from -1.5 to 1.5
- kv_weight: bfloat16 [3072, 3072], P('fsdp'), may hold values from -0.109375 to 0.109375
- kv_bias: float32 [3072], replicated, may hold values from -3 to 3
- key_gain: float32 [128], replicated, may hold values from 0.5 to 1.5
- img_query: bfloat16 [512, 192, 1536], P(('dp', 'fsdp')), may hold values from -256 to 256
- img_key: bfloat16 [512, 192, 1536], P(('dp', 'fsdp')), may hold values from -6 to 6
- img_value: bfloat16 [512, 192, 1536], P(('dp', 'fsdp')), may hold values from -6 to 6
- out_grad: bfloat16 [512, 192, 1536], P(('dp', 'fsdp')), may hold values from -6 to 6
Outputs:
- table_grad: float32 [4096, 3072], P('dp', 'fsdp')
Inputs may be any that keep to these rules, and one draw needn't show every extreme that they name: `concept_ids`: concept of each sample, some concepts far more common than others.
All inputs are finite; a program needn't handle non-finite values.
Results may differ from a plain program's by a relative error of at most 0.0083.
Values may be sent and summed in bfloat16 or wider, within the bound.
A program may use at most 64 MiB of HBM per device.

v0:
```python
import jax
import jax.numpy as jnp
from jax import lax
from jax.sharding import PartitionSpec as P

EPSILON = 1e-06


def layer_norm(values):
    centre = jnp.mean(values, -1, keepdims=True)
    spread = jnp.mean((values - centre) ** 2, -1, keepdims=True)
    inverse = lax.rsqrt(spread + EPSILON)
    return ((values - centre) * inverse, inverse[..., 0])


def shards(
    txt_tokens,
    concept_table,
    concept_ids,
    positions,
    timesteps,
    counts,
    mod_table,
    kv_weight,
    kv_bias,
    key_gain,
    img_query,
    img_key,
    img_value,
    out_grad,
):
    highest = lax.Precision.HIGHEST
    fsdp_size = lax.axis_size("fsdp")
    column = lax.axis_index("fsdp")
    tok_len = txt_tokens.shape[1]
    model_width = txt_tokens.shape[2]
    slice_width = kv_weight.shape[0]
    kv_width = kv_weight.shape[1]
    head_width = kv_width // 2
    head_dim = key_gain.shape[0]
    head_count = head_width // head_dim
    img_len = img_query.shape[1]
    bucket_count = mod_table.shape[0]
    root_dh = jnp.sqrt(jnp.float32(head_dim))
    table_hat, table_rstd = layer_norm(concept_table.astype(jnp.float32))
    table_part = lax.dynamic_slice_in_dim(
        table_hat.astype(jnp.bfloat16), column * slice_width, slice_width, 1
    )
    table_all = lax.all_gather(table_part, "dp", axis=0, tiled=True)
    own_hat = layer_norm(txt_tokens[0].astype(jnp.float32))[0].astype(jnp.bfloat16)
    labels = jnp.stack([concept_ids[0], positions[0], timesteps[0]])
    label_tile = jnp.tile(labels[None, :], (1, fsdp_size))
    token_cols, label_cols = (
        lax.all_to_all(own_hat, "fsdp", split_axis=1, concat_axis=0, tiled=True),
        lax.all_to_all(label_tile, "fsdp", split_axis=1, concat_axis=0, tiled=True),
    )
    group_ids = label_cols[:, 0]
    group_pos = label_cols[:, 1]
    group_time = label_cols[:, 2]
    concept_cols = jnp.take(table_all, group_ids, axis=0)
    token_cols = token_cols.reshape(fsdp_size, tok_len, slice_width)
    is_place = jnp.arange(tok_len, dtype=jnp.int32)[None, :] == group_pos[:, None]
    token_cols = jnp.where(is_place[:, :, None], concept_cols[:, None, :], token_cols)
    pick_time = (jnp.arange(bucket_count, dtype=jnp.int32)[None, :] == group_time[:, None]).astype(
        jnp.bfloat16
    )
    modulation = jnp.dot(
        pick_time,
        mod_table.reshape(bucket_count, 2 * slice_width),
        preferred_element_type=jnp.float32,
    )
    modulation = modulation.reshape(fsdp_size, 2, slice_width)
    shift_cols = modulation[:, 0]
    scale_cols = 1.0 + modulation[:, 1]
    modulated = (
        scale_cols[:, None, :] * token_cols.astype(jnp.float32) + shift_cols[:, None, :]
    ).astype(jnp.bfloat16)
    kv_terms = jnp.dot(
        modulated.reshape(fsdp_size * tok_len, slice_width),
        kv_weight,
        preferred_element_type=jnp.float32,
    )
    kv_terms = kv_terms.reshape(fsdp_size, tok_len, kv_width)
    weight_f = kv_weight.astype(jnp.float32)
    concept_f = concept_cols.astype(jnp.float32)
    side_rows = jnp.stack([scale_cols, scale_cols * concept_f], 1).reshape(
        fsdp_size * 2, slice_width
    )
    side_terms = jnp.dot(side_rows, weight_f, precision=highest).reshape(fsdp_size, 2, kv_width)
    all_terms = jnp.concatenate([kv_terms, side_terms], 1)
    row_block = all_terms.shape[1]
    all_terms = all_terms.reshape(fsdp_size * row_block, kv_width)
    own_rows = lax.psum_scatter(all_terms, "fsdp", scatter_dimension=0, tiled=True)
    kv_rows = own_rows[:tok_len] + kv_bias
    pos_pick = (jnp.arange(tok_len, dtype=jnp.int32) == positions[0]).astype(jnp.float32)
    key_raw = kv_rows[:, :head_width].reshape(tok_len, head_count, head_dim)
    key_inv = lax.rsqrt(jnp.mean(key_raw * key_raw, -1) + EPSILON)
    key_norm = (
        (key_raw * key_inv[..., None] * key_gain).astype(jnp.bfloat16).reshape(tok_len, head_width)
    )
    val_txt = kv_rows[:, head_width:].astype(jnp.bfloat16)
    keys_all = jnp.concatenate([key_norm, img_key[0]], 0).reshape(
        tok_len + img_len, head_count, head_dim
    )
    vals_all = jnp.concatenate([val_txt, img_value[0]], 0).reshape(
        tok_len + img_len, head_count, head_dim
    )
    queries = img_query[0].reshape(img_len, head_count, head_dim)
    scores = (
        jnp.einsum("qhd,khd->hqk", queries, keys_all, preferred_element_type=jnp.float32) / root_dh
    )
    row_top = jnp.max(scores, -1, keepdims=True)
    raised = jnp.exp(scores - row_top)
    prob_full = raised / jnp.sum(raised, -1, keepdims=True)
    prob_low = prob_full.astype(jnp.bfloat16)
    attended = jnp.einsum("hqk,khd->qhd", prob_low, vals_all, preferred_element_type=jnp.float32)
    grad_f = out_grad[0].reshape(img_len, head_count, head_dim).astype(jnp.float32)
    row_delta = jnp.einsum("qhd,qhd->hq", grad_f, attended)
    prob_pos = jnp.einsum("hqk,k->hq", prob_full[:, :, :tok_len], pos_pick, precision=highest)
    val_local = val_txt.reshape(tok_len, head_count, head_dim).astype(jnp.float32)
    val_pos = jnp.einsum("k,khd->hd", pos_pick, val_local, precision=highest)
    grad_prob = jnp.einsum("qhd,hd->hq", grad_f, val_pos, precision=highest)
    grad_score = prob_pos * (grad_prob - row_delta)
    grad_val = jnp.einsum("hq,qhd->hd", prob_pos, grad_f, precision=highest)
    grad_key = (
        jnp.einsum("hq,qhd->hd", grad_score, queries.astype(jnp.float32), precision=highest)
        / root_dh
    )
    raw_pos = jnp.einsum("k,khd->hd", pos_pick, key_raw, precision=highest)
    inv_pos = jnp.einsum("k,kh->h", pos_pick, key_inv, precision=highest)
    normed_key = raw_pos * inv_pos[:, None]
    grad_norm = grad_key * key_gain
    grad_raw = inv_pos[:, None] * (
        grad_norm - normed_key * jnp.mean(grad_norm * normed_key, -1, keepdims=True)
    )
    grad_kv = jnp.concatenate([grad_raw.reshape(head_width), grad_val.reshape(head_width)])[None, :]
    side_mean = (
        jnp.stack(
            [
                jnp.dot(grad_kv[0], own_rows[tok_len], precision=highest),
                jnp.dot(grad_kv[0], own_rows[tok_len + 1], precision=highest),
            ]
        )
        / model_width
    )
    grads_all, sides_all = (
        lax.all_gather(grad_kv, "fsdp", axis=0, tiled=True),
        lax.all_gather(side_mean[None, :], "fsdp", axis=0, tiled=True),
    )
    grad_cols = jnp.dot(grads_all, weight_f.T, precision=highest) * scale_cols
    row_grad = grad_cols - sides_all[:, 0:1] - concept_f * sides_all[:, 1:2]
    owner_scale = table_rstd / counts.astype(jnp.float32)
    conc_total = table_all.shape[0]
    one_hot = (jnp.arange(conc_total, dtype=jnp.int32)[:, None] == group_ids[None, :]).astype(
        jnp.float32
    )
    dense_rows = jnp.dot(one_hot, row_grad, precision=highest)
    owned_rows = lax.psum_scatter(dense_rows, "dp", scatter_dimension=0, tiled=True)
    return owned_rows * owner_scale[:, None]


def solution(mesh):
    placed = (
        P(("dp", "fsdp"), None, None),
        P("dp", None),
        P(("dp", "fsdp")),
        P(("dp", "fsdp")),
        P(("dp", "fsdp")),
        P("dp"),
        P(None, None, "fsdp"),
        P("fsdp", None),
        P(),
        P(),
        P(("dp", "fsdp"), None, None),
        P(("dp", "fsdp"), None, None),
        P(("dp", "fsdp"), None, None),
        P(("dp", "fsdp"), None, None),
    )
    return jax.shard_map(
        shards, mesh=mesh, in_specs=placed, out_specs=P("dp", "fsdp"), check_vma=False
    )
```

profile of v0, /device:TPU:2, one launch (start us, length us, event | category | flops | bytes accessed | tf_op | source)
XLA Modules:
  0.0 369.3 jit_solution(15416597220606547347)
XLA Ops:
  9.3 9.3 %all-to-all-start = ((s32[1,32,3]{2,0,1:T(1,128)}), s32[1,32,3]{2,0,1:T(1,128)S(1)}, u32[]{:S(2)}, u32[]{:S(2)}) async-start(s32[1,32,3]{2,0,1:T(1,128)} %tile.2), calls=%async_computation | async-start | bytes 32768 | tf_op jit(solution)/shard_map/all_to_all | solution.py:55
  20.5 1.7 convert_reduce_fusion
  22.3 2.1 multiply_reduce_fusion
  25.0 1.1 fusion.32
  26.1 39.8 %all_gather.9 = bf16[4096,96]{1,0:T(8,128)(2,1)S(1)} all-gather(bf16[256,96]{1,0:T(8,128)(2,1)S(1)} %fusion.32), channel_id=1, replica_groups=mesh['dp'=16,'fsdp'=32] {'dp'}, dimensions={0}, use_global_device_ids=true | all-gather | bytes 835584 | tf_op jit(solution)/shard_map/all_gather | solution.py:49
  67.1 7.4 %all-to-all-start.1 = ((bf16[8,32,96]{2,0,1:T(8,128)(2,1)}), bf16[8,32,96]{2,0,1:T(8,128)(2,1)S(1)}, u32[]{:S(2)}, u32[]{:S(2)}) async-start(bf16[8,32,96]{2,0,1:T(8,128)(2,1)} %fusion.34), calls=%async_computation.1 | async-start | bytes 131072 | tf_op jit(solution)/shard_map/all_to_all | solution.py:54
  77.8 3.0 all-to-all-done.1
  81.4 3.4 pad_maximum_fusion
  84.8 5.3 %reshape.229 = f32[320,3072]{1,0:T(8,128)} reshape(f32[32,10,3072]{2,1,0:T(8,128)} %pad_maximum_fusion) | data formatting | bytes 7864320 | tf_op jit(solution)/shard_map/reshape | solution.py:92
  90.2 1.0 copy-done.7
  92.8 2.2 reshape_squeeze.7
  95.0 1.3 dynamic-slice
  97.4 126.6 %all-reduce.3.cloned.1.call-done = f32[320,3072]{1,0:T(8,128)} async-done(((f32[320,3072]{1,0:T(8,128)}), f32[320,3072]{1,0:T(8,128)}) %all-reduce.3.cloned.1.call-update) | async-done | bytes 3932176
  225.7 2.5 fusion.79
  230.7 1.0 fusion.6
  231.9 2.1 fusion.26
  234.0 1.7 fusion.28
  236.9 1.0 constant_dynamic-slice_fusion.1
  238.6 1.4 fusion.68
  240.0 20.8 %all-gather.1 = f32[32,1,2]{2,1,0:T(1,128)S(1)} all-gather(f32[1,1,2]{2,1,0:T(1,128)S(1)} %fusion.68), channel_id=1, replica_groups=mesh['dp'=16,'fsdp'=32] {'fsdp'}, dimensions={0}, use_global_device_ids=true | all-gather | bytes 264 | tf_op jit(solution)/shard_map/all_gather | solution.py:148
  260.9 24.3 %all-gather = f32[98304]{0:T(1024)S(1)} all-gather(f32[3072]{0:T(1024)S(1)} %get-tuple-element.7), channel_id=2, replica_groups=mesh['dp'=16,'fsdp'=32] {'fsdp'}, dimensions={0}, use_global_device_ids=true | all-gather | bytes 405504 | tf_op jit(solution)/shard_map/all_gather | solution.py:147
  285.9 2.0 fusion.23
  287.9 73.0 %reduce-scatter.2.cloned.1.call-done = f32[256,96]{0,1:T(8,128)} async-done(((f32[4096,96]{0,1:T(8,128)}), f32[256,96]{0,1:T(8,128)}) %reduce-scatter.2.cloned.1.call-update) | async-done | bytes 98320 | tf_op jit(solution)/shard_map/reduce_scatter | solution.py:158
  360.9 1.5 broadcast_multiply_fusion
  (100 shorter events, 17.2 us)
Async XLA Ops:
  6.5 70.1 %copy-start = (bf16[96,3072]{1,0:T(8,128)(2,1)S(1)}, bf16[96,3072]{1,0:T(8,128)(2,1)}, u32[]{:S(2)}) copy-start(bf16[96,3072]{1,0:T(8,128)(2,1)} %param.21) | copy-start | bytes 1769476
  6.5 15.7 %copy-start.1 = (bf16[256,3072]{1,0:T(8,128)(2,1)S(1)}, bf16[256,3072]{1,0:T(8,128)(2,1)}, u32[]{:S(2)}) copy-start(bf16[256,3072]{1,0:T(8,128)(2,1)} %param.15) | copy-start | bytes 4718596
  9.3 57.8 %all-to-all-start = ((s32[1,32,3]{2,0,1:T(1,128)}), s32[1,32,3]{2,0,1:T(1,128)S(1)}, u32[]{:S(2)}, u32[]{:S(2)}) async-start(s32[1,32,3]{2,0,1:T(1,128)} %tile.2), calls=%async_computation | async-start | bytes 32768 | tf_op jit(solution)/shard_map/all_to_all | solution.py:55
  22.2 2.2 copy-start.18
  22.2 43.7 %copy-start.10 = (bf16[1,8,3072]{2,1,0:T(8,128)(2,1)S(1)}, bf16[1,8,3072]{2,1,0:T(8,128)(2,1)}, u32[]{:S(2)}) copy-start(bf16[1,8,3072]{2,1,0:T(8,128)(2,1)} %param.14) | copy-start | bytes 147460
  22.3 44.6 %copy-start.13 = (bf16[64,2,96]{2,1,0:T(2,128)(2,1)S(1)}, bf16[64,2,96]{2,1,0:T(2,128)(2,1)}, u32[]{:S(2)}) copy-start(bf16[64,2,96]{2,1,0:T(2,128)(2,1)} %param.20) | copy-start | bytes 73732
  67.1 13.7 %all-to-all-start.1 = ((bf16[8,32,96]{2,0,1:T(8,128)(2,1)}), bf16[8,32,96]{2,0,1:T(8,128)(2,1)S(1)}, u32[]{:S(2)}, u32[]{:S(2)}) async-start(bf16[8,32,96]{2,0,1:T(8,128)(2,1)} %fusion.34), calls=%async_computation.1 | async-start | bytes 131072 | tf_op jit(solution)/shard_map/all_to_all | solution.py:54
  74.5 149.5 %all-reduce.3.cloned.1.call-start = ((), (), s32[]{:S(2)}) async-start(), calls=%async_computation.4 | async-start | bytes 7864320
  76.0 0.6 copy-start.11
  90.1 1.1 copy-start.7
  90.1 1.5 copy-start.8
  90.1 2.1 copy-start.9
  90.1 270.8 %reduce-scatter.2.cloned.1.call-start = ((), (), s32[]{:S(2)}) async-start(), calls=%async_computation.3 | async-start | bytes 1671168 | tf_op jit(solution)/shard_map/reduce_scatter | solution.py:158
  91.6 133.6 %copy-start.4 = (bf16[192,12,128]{2,1,0:T(8,128)(2,1)}, bf16[192,12,128]{2,1,0:T(8,128)(2,1)S(1)}, u32[]{:S(2)}) copy-start(bf16[192,12,128]{2,1,0:T(8,128)(2,1)S(1)} %reshape_squeeze.6) | copy-start | bytes 1769476
  92.2 4.8 %copy-start.19 = (f32[128]{0:T(128)S(1)}, f32[128]{0:T(128)}, u32[]{:S(2)}) copy-start(f32[128]{0:T(128)} %param.23) | copy-start | bytes 1540
  92.6 131.4 %copy-start.14 = (f32[3072]{0:T(1024)S(1)}, f32[3072]{0:T(1024)}, u32[]{:S(2)}) copy-start(f32[3072]{0:T(1024)} %param.22) | copy-start | bytes 36868
  225.0 3.2 copy-start.5
  228.6 1.1 copy-start.2
  229.7 2.0 copy-start.6
  229.8 6.3 %copy-start.17 = (f32[128]{0:T(128)S(1)}, f32[128]{0:T(128)}, u32[]{:S(2)}) copy-start(f32[128]{0:T(128)} %broadcast_multiply_fusion.3) | copy-start | bytes 1540
  230.7 5.7 %copy-start.3 = (bf16[192,12,128]{2,1,0:T(8,128)(2,1)S(1)}, bf16[192,12,128]{2,1,0:T(8,128)(2,1)}, u32[]{:S(2)}) copy-start(bf16[192,12,128]{2,1,0:T(8,128)(2,1)} %reshape_squeeze.7) | copy-start | bytes 1769476
  230.7 54.6 %copy-start.12 = (f32[32,2,96]{2,0,1:T(8,128)S(1)}, f32[32,2,96]{2,0,1:T(8,128)}, u32[]{:S(2)}) copy-start(f32[32,2,96]{2,0,1:T(8,128)} %copy-done.11) | copy-start | bytes 73732
  231.7 54.2 %copy-start.16 = (s32[32]{0:T(128)S(1)}, s32[32]{0:T(128)}, u32[]{:S(2)}) copy-start(s32[32]{0:T(128)} %get-tuple-element.16) | copy-start | bytes 388
  285.2 75.7 %copy-start.15 = (f32[256]{0:T(256)S(1)}, f32[256]{0:T(256)}, u32[]{:S(2)}) copy-start(f32[256]{0:T(256)} %get-tuple-element.20) | copy-start | bytes 3076
Sparse Core Ops, SparseCore 0:
  90.2 133.7 all-reduce.2
  288.1 72.8 reduce-scatter.1
where the time goes:
time: 370 us; the launch traced here: 369 us
  waiting for transfers between devices  203 us (55%)
  blocking collectives  84.9 us (23%)
  other arithmetic  21 us (6%)
  starting transfers between devices  16.8 us (5%)
  local copies, waits for them, and re-layouts  16.7 us (5%)
  between operations  16.5 us (4%)
  matrix products  10.8 us (3%)
    unnamed x3, waiting for transfers between devices  127 us
    reduce_scatter x1, waiting for transfers between devices, shards(): lax.psum_scatter(dense_rows, 'dp', scatter_dimension=0, tiled=True)  73 us
    all_gather x1, blocking collectives, shards(): table_all = lax.all_gather(table_part, 'dp', axis=0, tiled=True)  39.8 us
    all_gather x1, blocking collectives, shards(): lax.all_gather(grad_kv, 'fsdp', axis=0, tiled=True)  24.3 us
    all_gather x1, blocking collectives, shards(): lax.all_gather(side_mean[None, :], 'fsdp', axis=0, tiled=True)  20.8 us
    all_to_all x1, starting transfers between devices, shards(): lax.all_to_all(label_tile, 'fsdp', split_axis=1, concat_axis=0, tiled=True)  9.32 us
  transfers between devices with their start and end apart: 4, of which 3 were waited for; matrix products, arithmetic and copies ran while one was open for 5% of the time, Pallas kernels for 0%

commit v1 on v0

--- a/solution.py
+++ b/solution.py
@@ -144,7 +144,9 @@
         / model_width
     )
     grads_all, sides_all = (
-        lax.all_gather(grad_kv, "fsdp", axis=0, tiled=True),
+        jnp.concatenate(
+            lax.all_to_all(jnp.stack([grad_kv] * lax.axis_size("fsdp")), "fsdp", 0, 0), axis=0
+        ),
         lax.all_gather(side_mean[None, :], "fsdp", axis=0, tiled=True),
     )
     grad_cols = jnp.dot(grads_all, weight_f.T, precision=highest) * scale_cols

time: 370 us -> 354 us (0.957)
  blocking collectives: 84.9 us -> 61.2 us
  starting transfers between devices: 16.8 us -> 23.6 us
    all_gather x1 -> x0, blocking collectives: 24.3 us -> none  [shards(): lax.all_gather(grad_kv, 'fsdp', axis=0, tiled=True)]
    all_to_all x0 -> x1, starting transfers between devices: none -> 6.62 us  [shards(): lax.all_to_all(jnp.stack([grad_kv] * lax.axis_size('fsdp')), 'fsdp', 0, 0)]
  transfers between devices with their start and end apart: 4 -> 5, of which waited for: 3 -> 3; matrix products, arithmetic and copies ran while one was open for 5% -> 5% of each run, Pallas kernels for 0% -> 0%
where the time goes in v1:
time: 354 us; the launch traced here: 353 us
  waiting for transfers between devices  202 us (57%)
  blocking collectives  61.2 us (17%)
  starting transfers between devices  23.6 us (7%)
  other arithmetic  20.9 us (6%)
  local copies, waits for them, and re-layouts  17.6 us (5%)
  between operations  16.5 us (5%)
  matrix products  10.7 us (3%)
    unnamed x3, waiting for transfers between devices  127 us
    reduce_scatter x1, waiting for transfers between devices, shards(): lax.psum_scatter(dense_rows, 'dp', scatter_dimension=0, tiled=True)  72.8 us
    all_gather x1, blocking collectives, shards(): table_all = lax.all_gather(table_part, 'dp', axis=0, tiled=True)  39.8 us
    all_gather x1, blocking collectives, shards(): lax.all_gather(side_mean[None, :], 'fsdp', axis=0, tiled=True)  21.3 us
    all_to_all x1, starting transfers between devices, shards(): lax.all_to_all(label_tile, 'fsdp', split_axis=1, concat_axis=0, tiled=True)  9.32 us
    all_to_all x1, starting transfers between devices, shards(): lax.all_to_all(own_hat, 'fsdp', split_axis=1, concat_axis=0, tiled=True)  7.39 us
  transfers between devices with their start and end apart: 5, of which 3 were waited for; matrix products, arithmetic and copies ran while one was open for 5% of the time, Pallas kernels for 0%

profile of v1, /device:TPU:2, one launch (start us, length us, event | category | flops | bytes accessed | tf_op | source)
XLA Modules:
  0.0 352.8 jit_solution(4657196009542717818)
XLA Ops:
  9.3 9.3 %all-to-all-start = ((s32[1,32,3]{2,0,1:T(1,128)}), s32[1,32,3]{2,0,1:T(1,128)S(1)}, u32[]{:S(2)}, u32[]{:S(2)}) async-start(s32[1,32,3]{2,0,1:T(1,128)} %tile.2), calls=%async_computation | async-start | bytes 32768 | tf_op jit(solution)/shard_map/all_to_all | solution.py:55
  20.5 1.7 convert_reduce_fusion
  22.3 2.1 multiply_reduce_fusion
  25.0 1.1 fusion.34
  26.1 39.8 %all_gather.6 = bf16[4096,96]{1,0:T(8,128)(2,1)S(1)} all-gather(bf16[256,96]{1,0:T(8,128)(2,1)S(1)} %fusion.34), channel_id=1, replica_groups=mesh['dp'=16,'fsdp'=32] {'dp'}, dimensions={0}, use_global_device_ids=true | all-gather | bytes 835584 | tf_op jit(solution)/shard_map/all_gather | solution.py:49
  67.1 7.4 %all-to-all-start.1 = ((bf16[8,32,96]{2,0,1:T(8,128)(2,1)}), bf16[8,32,96]{2,0,1:T(8,128)(2,1)S(1)}, u32[]{:S(2)}, u32[]{:S(2)}) async-start(bf16[8,32,96]{2,0,1:T(8,128)(2,1)} %fusion.36), calls=%async_computation.1 | async-start | bytes 131072 | tf_op jit(solution)/shard_map/all_to_all | solution.py:54
  78.0 2.9 all-to-all-done.1
  81.4 3.4 pad_maximum_fusion
  84.8 5.3 %reshape.234 = f32[320,3072]{1,0:T(8,128)} reshape(f32[32,10,3072]{2,1,0:T(8,128)} %pad_maximum_fusion) | data formatting | bytes 7864320 | tf_op jit(solution)/shard_map/reshape | solution.py:92
  90.1 1.0 copy-done.7
  92.8 2.2 reshape_squeeze.7
  95.0 1.3 dynamic-slice
  97.4 126.6 %all-reduce.3.cloned.1.call-done = f32[320,3072]{1,0:T(8,128)} async-done(((f32[320,3072]{1,0:T(8,128)}), f32[320,3072]{1,0:T(8,128)}) %all-reduce.3.cloned.1.call-update) | async-done | bytes 3932176
  225.7 2.5 fusion.81
  230.7 1.0 fusion.6
  231.9 2.1 fusion.26
  234.0 1.7 fusion.28
  236.9 1.0 constant_dynamic-slice_fusion.1
  239.5 6.6 %all-to-all-start.2 = ((f32[32,1,3072]{2,1,0:T(1,128)}), f32[32,1,3072]{2,1,0:T(1,128)S(1)}, u32[]{:S(2)}, u32[]{:S(2)}) async-start(f32[32,1,3072]{2,1,0:T(1,128)} %stack.22), calls=%async_computation.2 | async-start | bytes 786432 | tf_op jit(solution)/shard_map/all_to_all | solution.py:148
  246.2 1.3 fusion.70
  247.6 21.3 %all-gather = f32[32,1,2]{2,1,0:T(1,128)S(1)} all-gather(f32[1,1,2]{2,1,0:T(1,128)S(1)} %fusion.70), channel_id=1, replica_groups=mesh['dp'=16,'fsdp'=32] {'fsdp'}, dimensions={0}, use_global_device_ids=true | all-gather | bytes 264 | tf_op jit(solution)/shard_map/all_gather | solution.py:150
  269.6 2.0 fusion.23
  271.6 72.8 %reduce-scatter.2.cloned.1.call-done = f32[256,96]{0,1:T(8,128)} async-done(((f32[4096,96]{0,1:T(8,128)}), f32[256,96]{0,1:T(8,128)}) %reduce-scatter.2.cloned.1.call-update) | async-done | bytes 98320 | tf_op jit(solution)/shard_map/reduce_scatter | solution.py:160
  344.4 1.5 broadcast_multiply_fusion
  (101 shorter events, 18.2 us)
Async XLA Ops:
  6.5 70.3 %copy-start = (bf16[96,3072]{1,0:T(8,128)(2,1)S(1)}, bf16[96,3072]{1,0:T(8,128)(2,1)}, u32[]{:S(2)}) copy-start(bf16[96,3072]{1,0:T(8,128)(2,1)} %param.21) | copy-start | bytes 1769476
  6.5 15.7 %copy-start.1 = (bf16[256,3072]{1,0:T(8,128)(2,1)S(1)}, bf16[256,3072]{1,0:T(8,128)(2,1)}, u32[]{:S(2)}) copy-start(bf16[256,3072]{1,0:T(8,128)(2,1)} %param.15) | copy-start | bytes 4718596
  9.3 57.8 %all-to-all-start = ((s32[1,32,3]{2,0,1:T(1,128)}), s32[1,32,3]{2,0,1:T(1,128)S(1)}, u32[]{:S(2)}, u32[]{:S(2)}) async-start(s32[1,32,3]{2,0,1:T(1,128)} %tile.2), calls=%async_computation | async-start | bytes 32768 | tf_op jit(solution)/shard_map/all_to_all | solution.py:55
  22.2 2.2 copy-start.18
  22.2 43.7 %copy-start.10 = (bf16[1,8,3072]{2,1,0:T(8,128)(2,1)S(1)}, bf16[1,8,3072]{2,1,0:T(8,128)(2,1)}, u32[]{:S(2)}) copy-start(bf16[1,8,3072]{2,1,0:T(8,128)(2,1)} %param.14) | copy-start | bytes 147460
  22.3 44.6 %copy-start.13 = (bf16[64,2,96]{2,1,0:T(2,128)(2,1)S(1)}, bf16[64,2,96]{2,1,0:T(2,128)(2,1)}, u32[]{:S(2)}) copy-start(bf16[64,2,96]{2,1,0:T(2,128)(2,1)} %param.20) | copy-start | bytes 73732
  67.1 13.7 %all-to-all-start.1 = ((bf16[8,32,96]{2,0,1:T(8,128)(2,1)}), bf16[8,32,96]{2,0,1:T(8,128)(2,1)S(1)}, u32[]{:S(2)}, u32[]{:S(2)}) async-start(bf16[8,32,96]{2,0,1:T(8,128)(2,1)} %fusion.36), calls=%async_computation.1 | async-start | bytes 131072 | tf_op jit(solution)/shard_map/all_to_all | solution.py:54
  74.5 149.5 %all-reduce.3.cloned.1.call-start = ((), (), s32[]{:S(2)}) async-start(), calls=%async_computation.5 | async-start | bytes 7864320
  90.1 1.1 copy-start.7
  90.1 1.5 copy-start.8
  90.1 2.1 copy-start.9
  91.6 133.6 %copy-start.4 = (bf16[192,12,128]{2,1,0:T(8,128)(2,1)}, bf16[192,12,128]{2,1,0:T(8,128)(2,1)S(1)}, u32[]{:S(2)}) copy-start(bf16[192,12,128]{2,1,0:T(8,128)(2,1)S(1)} %reshape_squeeze.6) | copy-start | bytes 1769476
  92.2 4.8 %copy-start.19 = (f32[128]{0:T(128)S(1)}, f32[128]{0:T(128)}, u32[]{:S(2)}) copy-start(f32[128]{0:T(128)} %param.23) | copy-start | bytes 1540
  92.6 131.4 %copy-start.14 = (f32[3072]{0:T(1024)S(1)}, f32[3072]{0:T(1024)}, u32[]{:S(2)}) copy-start(f32[3072]{0:T(1024)} %param.22) | copy-start | bytes 36868
  225.0 3.2 copy-start.5
  228.6 1.1 copy-start.2
  229.7 2.0 copy-start.6
  229.8 6.3 %copy-start.17 = (f32[128]{0:T(128)S(1)}, f32[128]{0:T(128)}, u32[]{:S(2)}) copy-start(f32[128]{0:T(128)} %broadcast_multiply_fusion.3) | copy-start | bytes 1540
  230.7 5.7 %copy-start.3 = (bf16[192,12,128]{2,1,0:T(8,128)(2,1)S(1)}, bf16[192,12,128]{2,1,0:T(8,128)(2,1)}, u32[]{:S(2)}) copy-start(bf16[192,12,128]{2,1,0:T(8,128)(2,1)} %reshape_squeeze.7) | copy-start | bytes 1769476
  230.7 38.3 %copy-start.12 = (f32[32,2,96]{2,0,1:T(8,128)S(1)}, f32[32,2,96]{2,0,1:T(8,128)}, u32[]{:S(2)}) copy-start(f32[32,2,96]{2,0,1:T(8,128)} %copy-done.11) | copy-start | bytes 73732
  231.7 37.9 %copy-start.16 = (s32[32]{0:T(128)S(1)}, s32[32]{0:T(128)}, u32[]{:S(2)}) copy-start(s32[32]{0:T(128)} %get-tuple-element.16) | copy-start | bytes 388
  239.5 104.9 %copy-start.15 = (f32[256]{0:T(256)S(1)}, f32[256]{0:T(256)}, u32[]{:S(2)}) copy-start(f32[256]{0:T(256)} %get-tuple-element.20) | copy-start | bytes 3076
  239.5 29.4 %all-to-all-start.2 = ((f32[32,1,3072]{2,1,0:T(1,128)}), f32[32,1,3072]{2,1,0:T(1,128)S(1)}, u32[]{:S(2)}, u32[]{:S(2)}) async-start(f32[32,1,3072]{2,1,0:T(1,128)} %stack.22), calls=%async_computation.2 | async-start | bytes 786432 | tf_op jit(solution)/shard_map/all_to_all | solution.py:148
  246.2 98.2 %reduce-scatter.2.cloned.1.call-start = ((), (), s32[]{:S(2)}) async-start(), calls=%async_computation.4 | async-start | bytes 1671168 | tf_op jit(solution)/shard_map/reduce_scatter | solution.py:160
  (1 other events, 0.6 us)
Sparse Core Ops, SparseCore 0:
  90.2 133.7 all-reduce.2
  271.7 72.6 reduce-scatter.1
